TPU v7x, 32 devices: a whole 2x2x4 slice. The times are simulated.
32 devices in a mesh: cand: 4 (over y, core), hid: 8 (over z, x).
Axes of the slice: x: 2, y: 2, z: 4, core: 2. Of those that a mesh axis runs over, the one named last changes fastest.
Arguments:
- tokens: bfloat16 [4, 256, 2048], P('cand', None, 'hid'), may hold values from -6 to 6
- cotangent: bfloat16 [4, 256, 2048], P('cand', None, 'hid'), may hold values from -6 to 6
- gate_weight: bfloat16 [2048, 8192], P('cand', 'hid'), may hold values from -0.125 to 0.125
- up_weight: bfloat16 [2048, 8192], P('cand', 'hid'), may hold values from -0.125 to 0.125
- down_weight: bfloat16 [8192, 2048], P('hid', 'cand'), may hold values from -0.125 to 0.125
- width_steps: int32 [4], P('cand'), may hold values from 1 to 8
- block_order: int32 [8], replicated, may hold values from 0 to 7, each once
Outputs:
- grad_tokens: float32 [4, 256, 2048], P('cand', None, 'hid')
- grad_gate: float32 [2048, 8192], P('cand', 'hid')
- grad_up: float32 [2048, 8192], P('cand', 'hid')
- grad_down: float32 [8192, 2048], P('hid', 'cand')
Inputs may be any that keep to these rules, and one draw needn't show every extreme that they name: Candidate c uses the first width_steps[c] * 1024 logical hidden units. `block_order`: names each of the 8 logical blocks once.
All inputs are finite; a program needn't handle non-finite values.
Results may differ from a plain program's by a relative error of at most 0.02.
Values may be sent and summed in bfloat16 or wider, within the bound.
A program may use at most 64 MiB of HBM per device.

v0:
```python
import jax
import jax.numpy as jnp
from jax import lax
from jax.sharding import PartitionSpec as P

FF = 8192


def shards(tokens, cotangent, gate_weight, up_weight, down_weight, width_steps, block_order):
    inputs, upstream = (
        lax.all_gather(tokens, "hid", axis=2, tiled=True),
        lax.all_gather(cotangent, "hid", axis=2, tiled=True),
    )
    inputs = inputs[0]
    upstream = upstream[0]
    gate_full, up_full = (
        lax.all_gather(gate_weight, "cand", axis=0, tiled=True),
        lax.all_gather(up_weight, "cand", axis=0, tiled=True),
    )
    down_full = lax.all_gather(down_weight, "cand", axis=1, tiled=True)
    width = gate_weight.shape[1]
    places = jnp.arange(block_order.shape[0], dtype=jnp.int32)
    logical = jnp.sum(jnp.where(places == lax.axis_index("hid"), block_order, 0))
    active = logical * width < width_steps[0] * (FF // 8)
    keep = active.astype(jnp.float32)
    gate = jnp.dot(inputs, gate_full, preferred_element_type=jnp.float32)
    up = jnp.dot(inputs, up_full, preferred_element_type=jnp.float32)
    sig = jax.nn.sigmoid(gate)
    act = keep * gate * sig
    hidden = (act * up).astype(jnp.bfloat16)
    dhid = keep * jnp.einsum("td,fd->tf", upstream, down_full, preferred_element_type=jnp.float32)
    forward_d_up = (dhid * act).astype(jnp.bfloat16)
    forward_d_gate = (dhid * up * keep * sig * (1.0 + gate * (1.0 - sig))).astype(jnp.bfloat16)
    down_local = jnp.einsum("tf,td->fd", hidden, upstream, preferred_element_type=jnp.float32)
    down_local, d_gate, d_up = (down_local, forward_d_gate, forward_d_up)
    gate_local = jnp.einsum("td,tf->df", inputs, d_gate, preferred_element_type=jnp.float32)
    up_local = jnp.einsum("td,tf->df", inputs, d_up, preferred_element_type=jnp.float32)
    input_part = jnp.einsum("tf,df->td", d_gate, gate_full, preferred_element_type=jnp.float32)
    input_part = input_part + jnp.einsum(
        "tf,df->td", d_up, up_full, preferred_element_type=jnp.float32
    )
    gate_local, up_local, input_part = (gate_local, up_local, input_part)
    grad_tokens = lax.psum_scatter(
        input_part[None].astype(jnp.bfloat16), "hid", scatter_dimension=2, tiled=True
    ).astype(jnp.float32)
    grad_gate, grad_up = (
        lax.psum_scatter(
            gate_local.astype(jnp.bfloat16), "cand", scatter_dimension=0, tiled=True
        ).astype(jnp.float32),
        lax.psum_scatter(
            up_local.astype(jnp.bfloat16), "cand", scatter_dimension=0, tiled=True
        ).astype(jnp.float32),
    )
    grad_down = lax.psum_scatter(
        down_local.astype(jnp.bfloat16), "cand", scatter_dimension=1, tiled=True
    ).astype(jnp.float32)
    return (grad_tokens, grad_gate, grad_up, grad_down)


def solution(mesh):
    in_specs = (
        P("cand", None, "hid"),
        P("cand", None, "hid"),
        P("cand", "hid"),
        P("cand", "hid"),
        P("hid", "cand"),
        P("cand"),
        P(),
    )
    out_specs = (P("cand", None, "hid"), P("cand", "hid"), P("cand", "hid"), P("hid", "cand"))
    return jax.shard_map(shards, mesh=mesh, in_specs=in_specs, out_specs=out_specs, check_vma=False)
```

profile of v0, /device:TPU:0, one launch (start us, length us, event | category | flops | bytes accessed | tf_op | source)
XLA Modules:
  0.0 422.3 jit_solution(7583610765798703201)
XLA Ops:
  7.2 0.0 all-gather.10.cloned.1.call-start
  7.2 0.7 all-gather.10.cloned.1.call-update
  7.9 0.0 all-gather.12.cloned.1.call-start
  7.9 0.7 all-gather.12.cloned.1.call-update
  8.6 0.0 all-gather.14.cloned.1.call-start
  8.7 0.7 all-gather.14.cloned.1.call-update
  9.4 0.0 all-gather.6.cloned.1.call-start
  9.4 0.5 all-gather.6.cloned.1.call-update
  10.0 0.0 all-gather.8.cloned.1.call-start
  10.0 0.5 all-gather.8.cloned.1.call-update
  10.5 0.0 reduce-scatter.5.cloned.1.call-start
  11.2 1.3 fusion.10
  13.2 39.0 %all-gather.10.cloned.1.call-done = bf16[1,256,2048]{2,1,0:T(8,128)(2,1)} async-done(((bf16[1,256,256]{2,1,0:T(8,128)(2,1)}), bf16[1,256,2048]{2,1,0:T(8,128)(2,1)}) %all-gather.10.cloned.1.call-update) | async-done | bytes 1048592 | tf_op jit(solution)/shard_map/all_gather | solution.py:11
  52.2 0.0 copy-start
  52.2 35.1 %all-gather.12.cloned.1.call-done = bf16[2048,1024]{1,0:T(8,128)(2,1)} async-done(((bf16[512,1024]{1,0:T(8,128)(2,1)}), bf16[2048,1024]{1,0:T(8,128)(2,1)}) %all-gather.12.cloned.1.call-update) | async-done | bytes 4194320 | tf_op jit(solution)/shard_map/all_gather | solution.py:18
  87.2 3.8 fusion.6
  91.0 0.0 copy-start.4
  91.0 32.3 %all-gather.14.cloned.1.call-done = bf16[2048,1024]{1,0:T(8,128)(2,1)} async-done(((bf16[512,1024]{1,0:T(8,128)(2,1)}), bf16[2048,1024]{1,0:T(8,128)(2,1)}) %all-gather.14.cloned.1.call-update) | async-done | bytes 4194320 | tf_op jit(solution)/shard_map/all_gather | solution.py:17
  123.3 0.0 copy-done
  123.3 4.4 %fusion.4 = f32[256,1024]{1,0:T(8,128)} fusion(bf16[2048,1024]{1,0:T(8,128)(2,1)} %all-gather.14.cloned.1.call-done, bf16[1,256,2048]{2,1,0:T(8,128)(2,1)S(1)} %copy-done), kind=kOutput, calls=%fused_computation.9 | convolution fusion | flops 1073741824 | bytes 6291456 | tf_op jit(solution)/shard_map/dot_general | solution.py:26
  127.7 36.9 %all-gather.6.cloned.1.call-done = bf16[1,256,2048]{2,1,0:T(8,128)(2,1)} async-done(((bf16[1,256,256]{2,1,0:T(8,128)(2,1)}), bf16[1,256,2048]{2,1,0:T(8,128)(2,1)}) %all-gather.6.cloned.1.call-update) | async-done | bytes 1048592 | tf_op jit(solution)/shard_map/all_gather | solution.py:12
  164.6 34.9 %all-gather.8.cloned.1.call-done = bf16[1024,2048]{1,0:T(8,128)(2,1)} async-done(((bf16[1024,512]{1,0:T(8,128)(2,1)}), bf16[1024,2048]{1,0:T(8,128)(2,1)}) %all-gather.8.cloned.1.call-update) | async-done | bytes 4194320 | tf_op jit(solution)/shard_map/all_gather | solution.py:20
  199.5 4.6 %multiply_convert_fusion.1 = (bf16[256,1024]{1,0:T(8,128)(2,1)S(1)}, bf16[256,1024]{1,0:T(8,128)(2,1)S(1)}) fusion(f32[256,1024]{1,0:T(8,128)} %fusion.4, f32[]{:T(128)S(6)} %convert_element_type.45, f32[256,1024]{1,0:T(8,128)S(1)} %fusion.6, bf16[1024,2048]{1,0:T(8,128)(2,1)} %all-gather.8.cloned.1.call-done, ...), kind=kOutput, calls=%fused_computation.16 | convolution fusion | flops 1077936128 | bytes 8388612 | tf_op jit(solution)/shard_map/td,fd->tf/dot_general | solution.py:31
  204.1 0.0 copy-done.4
  204.1 0.0 copy-start.1
  204.1 0.0 copy-done.2
  204.2 1.3 fusion.12
  205.4 0.9 copy-done.1
  206.3 2.3 fusion.1
  208.6 0.0 reduce-scatter.5.cloned.1.call-update
  208.6 0.0 reduce-scatter.11.cloned.1.call-start
  208.7 0.0 copy-done.3
  208.7 4.9 %convolution_convert_fusion = bf16[1024,2048]{1,0:T(8,128)(2,1)} fusion(bf16[1,256,2048]{2,1,0:T(8,128)(2,1)S(1)} %copy-done.3, f32[256,1024]{1,0:T(8,128)} %copy-done.4, f32[256,1024]{1,0:T(8,128)} %fusion.4, f32[]{:T(128)S(6)} %convert_element_type.45), kind=kOutput, calls=%fused_computation.2 | convolution fusion | flops 1077673984 | bytes 7340036 | tf_op jit(solution)/shard_map/tf,td->fd/dot_general | solution.py:34
  213.5 0.0 reduce-scatter.11.cloned.1.call-update
  213.6 0.0 reduce-scatter.9.cloned.1.call-start
  213.6 3.3 convert_bitcast_fusion
  216.9 0.0 reduce-scatter.9.cloned.1.call-update
  216.9 0.0 reduce-scatter.7.cloned.1.call-start
  217.0 3.3 convert_bitcast_fusion.1
  220.2 0.0 reduce-scatter.7.cloned.1.call-update
  220.2 53.1 %reduce-scatter.5.cloned.1.call-done = bf16[1,256,256]{2,1,0:T(8,128)(2,1)} async-done(((bf16[1,256,2048]{2,1,0:T(8,128)(2,1)}), bf16[1,256,256]{2,1,0:T(8,128)(2,1)}) %reduce-scatter.5.cloned.1.call-update) | async-done | bytes 131088 | tf_op jit(solution)/shard_map/reduce_scatter | solution.py:43
  273.3 1.6 convert_element_type.50
  275.0 44.3 %reduce-scatter.11.cloned.1.call-done = bf16[1024,512]{1,0:T(8,128)(2,1)} async-done(((bf16[1024,2048]{1,0:T(8,128)(2,1)}), bf16[1024,512]{1,0:T(8,128)(2,1)}) %reduce-scatter.11.cloned.1.call-update) | async-done | bytes 1048592 | tf_op jit(solution)/shard_map/reduce_scatter | solution.py:54
  319.2 2.8 convert_element_type.59
  322.1 44.1 %reduce-scatter.9.cloned.1.call-done = bf16[512,1024]{0,1:T(8,128)(2,1)} async-done(((bf16[2048,1024]{0,1:T(8,128)(2,1)}), bf16[512,1024]{0,1:T(8,128)(2,1)}) %reduce-scatter.9.cloned.1.call-update) | async-done | bytes 1048592 | tf_op jit(solution)/shard_map/reduce_scatter | solution.py:50
  366.2 2.6 copy.12
  368.8 44.4 %reduce-scatter.7.cloned.1.call-done = bf16[512,1024]{0,1:T(8,128)(2,1)} async-done(((bf16[2048,1024]{0,1:T(8,128)(2,1)}), bf16[512,1024]{0,1:T(8,128)(2,1)}) %reduce-scatter.7.cloned.1.call-update) | async-done | bytes 1048592 | tf_op jit(solution)/shard_map/reduce_scatter | solution.py:47
  413.2 2.6 copy.11
  (2 shorter events, 0.0 us)
Async XLA Ops:
  7.2 45.0 %all-gather.10.cloned.1.call-start = ((), (), s32[]{:S(2)}) async-start(), calls=%async_computation.6 | async-start | bytes 1179648 | tf_op jit(solution)/shard_map/all_gather | solution.py:11
  7.9 79.3 %all-gather.12.cloned.1.call-start = ((), (), s32[]{:S(2)}) async-start(), calls=%async_computation.7 | async-start | bytes 5242880 | tf_op jit(solution)/shard_map/all_gather | solution.py:18
  8.6 114.6 %all-gather.14.cloned.1.call-start = ((), (), s32[]{:S(2)}) async-start(), calls=%async_computation.8 | async-start | bytes 5242880 | tf_op jit(solution)/shard_map/all_gather | solution.py:17
  9.4 155.2 %all-gather.6.cloned.1.call-start = ((), (), s32[]{:S(2)}) async-start(), calls=%async_computation.4 | async-start | bytes 1179648 | tf_op jit(solution)/shard_map/all_gather | solution.py:12
  10.0 189.6 %all-gather.8.cloned.1.call-start = ((), (), s32[]{:S(2)}) async-start(), calls=%async_computation.5 | async-start | bytes 5242880 | tf_op jit(solution)/shard_map/all_gather | solution.py:20
  10.5 262.8 %reduce-scatter.5.cloned.1.call-start = ((), (), s32[]{:S(2)}) async-start(), calls=%async_computation.9 | async-start | bytes 1179648 | tf_op jit(solution)/shard_map/reduce_scatter | solution.py:43
  52.2 71.1 %copy-start = (bf16[1,256,2048]{2,1,0:T(8,128)(2,1)S(1)}, bf16[1,256,2048]{2,1,0:T(8,128)(2,1)}, u32[]{:S(2)}) copy-start(bf16[1,256,2048]{2,1,0:T(8,128)(2,1)} %all-gather.10.cloned.1.call-done) | copy-start | bytes 3145732
  91.0 113.1 %copy-start.4 = (f32[256,1024]{1,0:T(8,128)}, f32[256,1024]{1,0:T(8,128)S(1)}, u32[]{:S(2)}) copy-start(f32[256,1024]{1,0:T(8,128)S(1)} %fusion.6) | copy-start | bytes 3145732
  199.5 4.6 %copy-start.2 = (bf16[2048,1024]{1,0:T(8,128)(2,1)S(1)}, bf16[2048,1024]{1,0:T(8,128)(2,1)}, u32[]{:S(2)}) copy-start(bf16[2048,1024]{1,0:T(8,128)(2,1)} %all-gather.14.cloned.1.call-done) | copy-start | bytes 12582916
  204.1 2.2 copy-start.1
  206.3 2.3 copy-start.3
  208.6 110.6 %reduce-scatter.11.cloned.1.call-start = ((), (), s32[]{:S(2)}) async-start(), calls=%async_computation.12 | async-start | bytes 5242880 | tf_op jit(solution)/shard_map/reduce_scatter | solution.py:54
  213.6 152.6 %reduce-scatter.9.cloned.1.call-start = ((), (), s32[]{:S(2)}) async-start(), calls=%async_computation.11 | async-start | bytes 5242880 | tf_op jit(solution)/shard_map/reduce_scatter | solution.py:50
  216.9 196.3 %reduce-scatter.7.cloned.1.call-start = ((), (), s32[]{:S(2)}) async-start(), calls=%async_computation.10 | async-start | bytes 5242880 | tf_op jit(solution)/shard_map/reduce_scatter | solution.py:47
Sparse Core Ops, SparseCore 0:
  10.0 42.1 all-gather.9
  53.7 33.4 all-gather.11
  88.8 34.4 all-gather.13
  125.2 39.3 all-gather.5
  166.0 33.4 all-gather.7
  208.7 64.5 reduce-scatter.4
  275.9 43.3 reduce-scatter.10
  321.8 44.3 reduce-scatter.8
  368.7 44.3 reduce-scatter.6
where the time goes:
time: 423 us; the launch traced here: 422 us
  waiting for transfers between devices  367 us (87%)
  matrix products  27.7 us (7%)
  between operations  15.2 us (4%)
  local copies, waits for them, and re-layouts  6.02 us (1%)
  other arithmetic  5.75 us (1%)
    reduce_scatter x1, waiting for transfers between devices, shards(): lax.psum_scatter(input_part[None].astype(jnp.bfloat16), 'hid', scatter_di...  53.1 us
    reduce_scatter x1, waiting for transfers between devices, shards(): lax.psum_scatter(gate_local.astype(jnp.bfloat16), 'cand', scatter_dimensi...  44.4 us
    reduce_scatter x1, waiting for transfers between devices, shards(): lax.psum_scatter(down_local.astype(jnp.bfloat16), 'cand', scatter_dimensi...  44.3 us
    reduce_scatter x1, waiting for transfers between devices, shards(): lax.psum_scatter(up_local.astype(jnp.bfloat16), 'cand', scatter_dimension...  44.1 us
    all_gather x1, waiting for transfers between devices, shards(): lax.all_gather(tokens, 'hid', axis=2, tiled=True)  39 us
    all_gather x1, waiting for transfers between devices, shards(): lax.all_gather(cotangent, 'hid', axis=2, tiled=True)  36.9 us
    all_gather x1, waiting for transfers between devices, shards(): lax.all_gather(up_weight, 'cand', axis=0, tiled=True)  35.1 us
    all_gather x1, waiting for transfers between devices, shards(): down_full = lax.all_gather(down_weight, 'cand', axis=1, tiled=True)  34.9 us
  transfers between devices with their start and end apart: 9, of which 9 were waited for; matrix products, arithmetic and copies ran while one was open for 7% of the time, Pallas kernels for 0%

commit v1 on v0

--- a/solution.py
+++ b/solution.py
@@ -7,6 +7,20 @@
 
 
 def shards(tokens, cotangent, gate_weight, up_weight, down_weight, width_steps, block_order):
+
+    def see_zone(unit, shard_in):
+        even = lax.axis_size("cand")
+        side_arr = lax.axis_index("cand")
+        piece_next, g_now, built = (even, side_arr, unit.shape[1])
+        fields = [(nth, (nth + 1) % piece_next) for nth in range(piece_next)]
+        w_next, taken_in = (unit, None)
+        for k0 in [*range(piece_next)]:
+            oldest = lax.ppermute(w_next, "cand", fields) if k0 < piece_next - 1 else None
+            t_next = shard_in(w_next, (g_now - k0) % piece_next * built)
+            taken_in = t_next if taken_in is None else taken_in + t_next
+            w_next = oldest
+        return taken_in
+
     inputs, upstream = (
         lax.all_gather(tokens, "hid", axis=2, tiled=True),
         lax.all_gather(cotangent, "hid", axis=2, tiled=True),
@@ -17,7 +31,6 @@
         lax.all_gather(gate_weight, "cand", axis=0, tiled=True),
         lax.all_gather(up_weight, "cand", axis=0, tiled=True),
     )
-    down_full = lax.all_gather(down_weight, "cand", axis=1, tiled=True)
     width = gate_weight.shape[1]
     places = jnp.arange(block_order.shape[0], dtype=jnp.int32)
     logical = jnp.sum(jnp.where(places == lax.axis_index("hid"), block_order, 0))
@@ -28,7 +41,15 @@
     sig = jax.nn.sigmoid(gate)
     act = keep * gate * sig
     hidden = (act * up).astype(jnp.bfloat16)
-    dhid = keep * jnp.einsum("td,fd->tf", upstream, down_full, preferred_element_type=jnp.float32)
+    dhid = keep * see_zone(
+        down_weight,
+        shard_in=lambda own_block, start: jnp.einsum(
+            "td,fd->tf",
+            lax.dynamic_slice_in_dim(upstream, start, own_block.shape[1], axis=1),
+            own_block,
+            preferred_element_type=jnp.float32,
+        ),
+    )
     forward_d_up = (dhid * act).astype(jnp.bfloat16)
     forward_d_gate = (dhid * up * keep * sig * (1.0 + gate * (1.0 - sig))).astype(jnp.bfloat16)
     down_local = jnp.einsum("tf,td->fd", hidden, upstream, preferred_element_type=jnp.float32)

time: 423 us -> 389 us (0.920)
  waiting for transfers between devices: 367 us -> 330 us
    all_gather x1 -> x0, waiting for transfers between devices: 34.9 us -> none  [shards(): down_full = lax.all_gather(down_weight, 'cand', axis=1, tiled=True)]
    ppermute x0 -> x3, waiting for transfers between devices: none -> 14.6 us  [see_zone(): lax.ppermute(w_next, 'cand', fields)]
    all_gather x1, waiting for transfers between devices: 36.9 us -> 24.3 us  [shards(): lax.all_gather(cotangent, 'hid', axis=2, tiled=True)]
  transfers between devices with their start and end apart: 9 -> 11, of which waited for: 9 -> 9; matrix products, arithmetic and copies ran while one was open for 7% -> 8% of each run, Pallas kernels for 0% -> 0%
where the time goes in v1:
time: 389 us
  waiting for transfers between devices  330 us (85%)
  matrix products  28.9 us (7%)
  between operations  15.6 us (4%)
  local copies, waits for them, and re-layouts  7.6 us (2%)
  other arithmetic  5.75 us (1%)
    reduce_scatter x1, waiting for transfers between devices, shards(): lax.psum_scatter(input_part[None].astype(jnp.bfloat16), 'hid', scatter_di...  53.3 us
    reduce_scatter x1, waiting for transfers between devices, shards(): lax.psum_scatter(up_local.astype(jnp.bfloat16), 'cand', scatter_dimension...  44.4 us
    reduce_scatter x1, waiting for transfers between devices, shards(): lax.psum_scatter(down_local.astype(jnp.bfloat16), 'cand', scatter_dimensi...  44.4 us
    reduce_scatter x1, waiting for transfers between devices, shards(): lax.psum_scatter(gate_local.astype(jnp.bfloat16), 'cand', scatter_dimensi...  44.1 us
    all_gather x1, waiting for transfers between devices, shards(): lax.all_gather(tokens, 'hid', axis=2, tiled=True)  35.8 us
    all_gather x1, waiting for transfers between devices, shards(): lax.all_gather(gate_weight, 'cand', axis=0, tiled=True)  35.1 us
    all_gather x1, waiting for transfers between devices, shards(): lax.all_gather(up_weight, 'cand', axis=0, tiled=True)  31.2 us
    all_gather x1, waiting for transfers between devices, shards(): lax.all_gather(cotangent, 'hid', axis=2, tiled=True)  24.3 us
  transfers between devices with their start and end apart: 11, of which 9 were waited for; matrix products, arithmetic and copies ran while one was open for 8% of the time, Pallas kernels for 0%

profile of v1, /device:TPU:0, one launch (start us, length us, event | category | flops | bytes accessed | tf_op | source)
XLA Modules:
  0.0 388.6 jit_solution(6391795120514430836)
XLA Ops:
  7.2 0.0 all-gather.5.cloned.1.call-start
  7.2 0.7 all-gather.5.cloned.1.call-update
  7.9 0.0 all-gather.7.cloned.1.call-start
  7.9 0.7 all-gather.7.cloned.1.call-update
  8.6 0.0 all-gather.11.cloned.1.call-start
  8.7 0.7 all-gather.11.cloned.1.call-update
  9.4 0.0 all-gather.9.cloned.1.call-start
  9.4 0.5 all-gather.9.cloned.1.call-update
  10.0 0.0 reduce-scatter.5.cloned.1.call-start
  10.0 0.5 collective-permute-start
  10.6 14.6 %collective-permute-done = bf16[1024,512]{1,0:T(8,128)(2,1)S(1)} collective-permute-done((bf16[1024,512]{1,0:T(8,128)(2,1)}, bf16[1024,512]{1,0:T(8,128)(2,1)S(1)}, u32[]{:S(2)}, u32[]{:S(2)}) %collective-permute-start) | collective-permute-done | bytes 1048608 | tf_op jit(solution)/shard_map/ppermute | solution.py:18
  25.2 0.0 collective-permute-start.1
  25.9 1.3 fusion.23
  27.9 24.3 %all-gather.5.cloned.1.call-done = bf16[1,256,2048]{2,1,0:T(8,128)(2,1)} async-done(((bf16[1,256,256]{2,1,0:T(8,128)(2,1)}), bf16[1,256,2048]{2,1,0:T(8,128)(2,1)}) %all-gather.5.cloned.1.call-update) | async-done | bytes 1048592 | tf_op jit(solution)/shard_map/all_gather | solution.py:26
  52.2 1.8 fusion.13
  53.9 1.4 convolution_add_fusion.3
  55.4 0.1 collective-permute-start.2
  55.5 1.4 convolution_add_fusion.2
  56.9 35.8 %all-gather.7.cloned.1.call-done = bf16[1,256,2048]{2,1,0:T(8,128)(2,1)} async-done(((bf16[1,256,256]{2,1,0:T(8,128)(2,1)}), bf16[1,256,2048]{2,1,0:T(8,128)(2,1)}) %all-gather.7.cloned.1.call-update) | async-done | bytes 1048592 | tf_op jit(solution)/shard_map/all_gather | solution.py:25
  92.7 35.1 %all-gather.11.cloned.1.call-done = bf16[2048,1024]{1,0:T(8,128)(2,1)} async-done(((bf16[512,1024]{1,0:T(8,128)(2,1)}), bf16[2048,1024]{1,0:T(8,128)(2,1)}) %all-gather.11.cloned.1.call-update) | async-done | bytes 4194320 | tf_op jit(solution)/shard_map/all_gather | solution.py:31
  127.7 4.7 %fusion.6 = f32[256,1024]{1,0:T(8,128)} fusion(bf16[2048,1024]{1,0:T(8,128)(2,1)} %all-gather.11.cloned.1.call-done, bf16[1,256,2048]{2,1,0:T(8,128)(2,1)} %all-gather.7.cloned.1.call-done), kind=kOutput, calls=%fused_computation.13 | convolution fusion | flops 1073741824 | bytes 6291456 | tf_op jit(solution)/shard_map/dot_general | solution.py:39
  132.5 31.2 %all-gather.9.cloned.1.call-done = bf16[2048,1024]{1,0:T(8,128)(2,1)} async-done(((bf16[512,1024]{1,0:T(8,128)(2,1)}), bf16[2048,1024]{1,0:T(8,128)(2,1)}) %all-gather.9.cloned.1.call-update) | async-done | bytes 4194320 | tf_op jit(solution)/shard_map/all_gather | solution.py:32
  163.6 3.5 fusion.8
  167.2 2.6 multiply_convert_fusion.1
  169.8 0.3 copy-done.2
  170.1 1.3 fusion.25
  171.4 0.6 copy-done.3
  172.1 2.3 fusion.1
  174.3 0.0 reduce-scatter.5.cloned.1.call-update
  174.4 0.0 reduce-scatter.7.cloned.1.call-start
  174.4 3.2 convert_bitcast_fusion.1
  177.6 0.0 reduce-scatter.7.cloned.1.call-update
  177.7 0.0 reduce-scatter.9.cloned.1.call-start
  177.7 3.3 convert_bitcast_fusion
  181.0 0.0 reduce-scatter.9.cloned.1.call-update
  181.0 0.0 reduce-scatter.11.cloned.1.call-start
  181.1 1.2 copy-done.5
  182.3 0.3 copy-done.7
  182.6 3.3 convolution_convert_fusion
  185.9 0.0 reduce-scatter.11.cloned.1.call-update
  185.9 53.3 %reduce-scatter.5.cloned.1.call-done = bf16[1,256,256]{2,1,0:T(8,128)(2,1)} async-done(((bf16[1,256,2048]{2,1,0:T(8,128)(2,1)}), bf16[1,256,256]{2,1,0:T(8,128)(2,1)}) %reduce-scatter.5.cloned.1.call-update) | async-done | bytes 131088 | tf_op jit(solution)/shard_map/reduce_scatter | solution.py:64
  239.2 1.6 convert_element_type.50
  240.9 44.1 %reduce-scatter.7.cloned.1.call-done = bf16[512,1024]{0,1:T(8,128)(2,1)} async-done(((bf16[2048,1024]{0,1:T(8,128)(2,1)}), bf16[512,1024]{0,1:T(8,128)(2,1)}) %reduce-scatter.7.cloned.1.call-update) | async-done | bytes 1048592 | tf_op jit(solution)/shard_map/reduce_scatter | solution.py:68
  285.0 2.6 copy.11
  287.6 44.4 %reduce-scatter.9.cloned.1.call-done = bf16[512,1024]{0,1:T(8,128)(2,1)} async-done(((bf16[2048,1024]{0,1:T(8,128)(2,1)}), bf16[512,1024]{0,1:T(8,128)(2,1)}) %reduce-scatter.9.cloned.1.call-update) | async-done | bytes 1048592 | tf_op jit(solution)/shard_map/reduce_scatter | solution.py:71
  331.9 2.6 copy.12
  334.5 44.4 %reduce-scatter.11.cloned.1.call-done = bf16[1024,512]{1,0:T(8,128)(2,1)} async-done(((bf16[1024,2048]{1,0:T(8,128)(2,1)}), bf16[1024,512]{1,0:T(8,128)(2,1)}) %reduce-scatter.11.cloned.1.call-update) | async-done | bytes 1048592 | tf_op jit(solution)/shard_map/reduce_scatter | solution.py:75
  378.9 2.8 convert_element_type.59
  (14 shorter events, 0.0 us)
Async XLA Ops:
  7.2 45.0 %all-gather.5.cloned.1.call-start = ((), (), s32[]{:S(2)}) async-start(), calls=%async_computation.4 | async-start | bytes 1179648 | tf_op jit(solution)/shard_map/all_gather | solution.py:26
  7.9 84.8 %all-gather.7.cloned.1.call-start = ((), (), s32[]{:S(2)}) async-start(), calls=%async_computation.5 | async-start | bytes 1179648 | tf_op jit(solution)/shard_map/all_gather | solution.py:25
  8.6 119.1 %all-gather.11.cloned.1.call-start = ((), (), s32[]{:S(2)}) async-start(), calls=%async_computation.7 | async-start | bytes 5242880 | tf_op jit(solution)/shard_map/all_gather | solution.py:31
  9.4 154.3 %all-gather.9.cloned.1.call-start = ((), (), s32[]{:S(2)}) async-start(), calls=%async_computation.6 | async-start | bytes 5242880 | tf_op jit(solution)/shard_map/all_gather | solution.py:32
  10.0 229.3 %reduce-scatter.5.cloned.1.call-start = ((), (), s32[]{:S(2)}) async-start(), calls=%async_computation.8 | async-start | bytes 1179648 | tf_op jit(solution)/shard_map/reduce_scatter | solution.py:64
  10.0 15.2 %collective-permute-start = (bf16[1024,512]{1,0:T(8,128)(2,1)}, bf16[1024,512]{1,0:T(8,128)(2,1)S(1)}, u32[]{:S(2)}, u32[]{:S(2)}) collective-permute-start(bf16[1024,512]{1,0:T(8,128)(2,1)} %param.11), channel_id=1, source_target_pairs={{0,8},{8,16},{16,24},{24,0},{1,9},{9,17},{17,25},{25,1},{2,10},{10... | collective-permute-start | bytes 3145736 | tf_op jit(solution)/shard_map/ppermute | solution.py:18
  25.2 30.2 %collective-permute-start.1 = (bf16[1024,512]{1,0:T(8,128)(2,1)S(1)}, bf16[1024,512]{1,0:T(8,128)(2,1)S(1)}, u32[]{:S(2)}, u32[]{:S(2)}) collective-permute-start(bf16[1024,512]{1,0:T(8,128)(2,1)S(1)} %collective-permute-done), channel_id=1, source_target_pairs={{0,8},{8,16},{16,24},{24,0},{1,9},{9,17},{17,25},{25,1},{2,10},{10... | collective-permute-start | bytes 3145736 | tf_op jit(solution)/shard_map/ppermute | solution.py:18
  55.4 111.8 %collective-permute-start.2 = (bf16[1024,512]{1,0:T(8,128)(2,1)S(1)}, bf16[1024,512]{1,0:T(8,128)(2,1)}, u32[]{:S(2)}, u32[]{:S(2)}) collective-permute-start(bf16[1024,512]{1,0:T(8,128)(2,1)S(1)} %collective-permute-done.1), channel_id=1, source_target_pairs={{0,8},{8,16},{16,24},{24,0},{1,9},{9,17},{17,25},{25,1},{2,10},{10... | collective-permute-start | bytes 3145736 | tf_op jit(solution)/shard_map/ppermute | solution.py:18
  92.7 71.0 %copy-start = (bf16[1,256,2048]{2,1,0:T(8,128)(2,1)S(1)}, bf16[1,256,2048]{2,1,0:T(8,128)(2,1)}, u32[]{:S(2)}) copy-start(bf16[1,256,2048]{2,1,0:T(8,128)(2,1)} %all-gather.7.cloned.1.call-done) | copy-start | bytes 3145732
  163.6 3.6 copy-start.4
  167.2 2.6 copy-start.6
  167.2 3.0 copy-start.2
  169.8 2.3 copy-start.3
  174.4 110.6 %reduce-scatter.7.cloned.1.call-start = ((), (), s32[]{:S(2)}) async-start(), calls=%async_computation.9 | async-start | bytes 5242880 | tf_op jit(solution)/shard_map/reduce_scatter | solution.py:68
  177.7 3.4 copy-start.1
  177.7 154.3 %reduce-scatter.9.cloned.1.call-start = ((), (), s32[]{:S(2)}) async-start(), calls=%async_computation.10 | async-start | bytes 5242880 | tf_op jit(solution)/shard_map/reduce_scatter | solution.py:71
  181.0 1.2 copy-start.5
  181.0 1.6 copy-start.7
  181.0 197.9 %reduce-scatter.11.cloned.1.call-start = ((), (), s32[]{:S(2)}) async-start(), calls=%async_computation.11 | async-start | bytes 5242880 | tf_op jit(solution)/shard_map/reduce_scatter | solution.py:75
Sparse Core Ops, SparseCore 0:
  10.0 42.1 all-gather.4
  54.2 38.3 all-gather.6
  94.2 33.4 all-gather.10
  129.1 34.4 all-gather.8
  174.5 64.7 reduce-scatter.4
  241.6 43.3 reduce-scatter.6
  287.5 44.3 reduce-scatter.8
  334.5 44.3 reduce-scatter.10
